TPU v7x, 512 devices: a whole 4x8x8 slice. The times are simulated.
512 devices in a mesh: fsdp: 32 (over z_hi, x, core), seq: 16 (over z_lo, y).
Axes of the slice: x: 4, y: 8, z: 8 (z_hi: 4, z_lo: 2; z = z_hi * 2 + z_lo), core: 2. Of those that a mesh axis runs over, the one named last changes fastest.
Arguments:
- video_qkv: bfloat16 [32, 2048, 3, 4096], P('fsdp', 'seq'), may hold values from -6 to 6
- reference_rows: bfloat16 [32, 64, 5120], P('fsdp', 'seq'), may hold values from -150 to 150
- kv_weight: bfloat16 [5120, 2, 4096], P('fsdp', None, 'seq'), may hold values from -0.125 to 0.125
- pose_table: bfloat16 [256, 4096], P('fsdp', 'seq'), may hold values from -6 to 6
- pose_ids: int32 [32, 2048], P('fsdp', 'seq'), may hold values from 0 to 255
- frame_counts: int32 [32], P('fsdp'), may hold values from 1 to 4, as said below
Outputs:
- attended: bfloat16 [32, 2048, 4096], P('fsdp', 'seq')
Inputs may be any that keep to these rules, and one draw needn't show every extreme that they name: `frame_counts`: every clip has 1 to 4 reference frames in the window, each making 16 slots live; in every draw some clip has exactly 4 and another exactly 1.
All inputs are finite; a program needn't handle non-finite values.
Results may differ from a plain program's by a relative error of at most 0.011.
Values may be sent and summed in bfloat16 or wider, within the bound.
No kernel may reach another device: no remote copies, remote signals or barrier semaphores. Data moves between devices by JAX's collectives and lax.ppermute only.
A program may use at most 64 MiB of HBM per device.

v0:
```python
import math
import jax
import jax.numpy as jnp
from jax import lax
from jax.sharding import PartitionSpec as P

HD = 128
TPF = 16
POSE = 256


def layer_norm(row_block):
    row_mean = jnp.mean(row_block, axis=-1, keepdims=True)
    centered = row_block - row_mean
    row_var = jnp.mean(centered * centered, axis=-1, keepdims=True)
    return centered * lax.rsqrt(row_var + 1e-06)


def pose_lookup(token_ids, codebook):
    onehot = (token_ids[:, None] == jnp.arange(POSE, dtype=jnp.int32)[None, :]).astype(jnp.bfloat16)
    return jnp.dot(onehot, codebook, preferred_element_type=jnp.float32)


def shards(video_qkv, reference_rows, kv_weight, pose_table, pose_ids, frame_counts):
    score_scale = 1.0 / math.sqrt(HD)
    query_part = video_qkv[:, :, 0:1, :]
    pair_part = video_qkv[:, :, 1:3, :]
    codebook_cols = lax.all_gather(pose_table, "seq", axis=1, tiled=True)
    codebook = lax.all_gather(codebook_cols, "fsdp", axis=0, tiled=True)
    lookup = pose_lookup(pose_ids[0], codebook)
    query_part = (query_part.astype(jnp.float32) + lookup[None, :, None, :]).astype(jnp.bfloat16)
    query_heads, pair_heads = (
        lax.all_to_all(query_part, "seq", split_axis=3, concat_axis=1, tiled=True),
        lax.all_to_all(pair_part, "seq", split_axis=3, concat_axis=1, tiled=True),
    )
    normed = layer_norm(reference_rows[0].astype(jnp.float32)).astype(jnp.bfloat16)
    all_rows = lax.all_gather(normed, "seq", axis=0, tiled=True)
    ref_count = all_rows.shape[0]
    head_width = kv_weight.shape[2]
    piece = lax.all_gather(kv_weight, "fsdp", axis=0, tiled=True)
    kv_sum = jnp.dot(
        all_rows, piece.reshape(piece.shape[0], 2 * head_width), preferred_element_type=jnp.float32
    )
    ref_kv = kv_sum.astype(jnp.bfloat16).reshape(ref_count, 2, head_width)
    video_len = query_heads.shape[1]
    heads_here = head_width // HD
    key_total = video_len + ref_count
    key_rows = jnp.concatenate([pair_heads[0, :, 0, :], ref_kv[:, 0, :]], axis=0).reshape(
        key_total, heads_here, HD
    )
    value_rows = jnp.concatenate([pair_heads[0, :, 1, :], ref_kv[:, 1, :]], axis=0).reshape(
        key_total, heads_here, HD
    )
    live_keys = jnp.arange(key_total, dtype=jnp.int32) < video_len + TPF * frame_counts[0]
    block_rows = min(512, video_len)
    block_count = video_len // block_rows

    def attend(query_block):
        scores = (
            jnp.einsum("bhd,khd->hbk", query_block, key_rows, preferred_element_type=jnp.float32)
            * score_scale
        )
        scores = jnp.where(live_keys[None, None, :], scores, -1e30)
        row_max = jnp.max(scores, axis=-1, keepdims=True)
        expo = jnp.where(live_keys[None, None, :], jnp.exp(scores - row_max), 0.0)
        row_total = jnp.sum(expo, axis=-1, keepdims=True)
        weights = (expo / row_total).astype(jnp.bfloat16)
        mixed = jnp.einsum("hbk,khd->bhd", weights, value_rows, preferred_element_type=jnp.float32)
        return mixed.astype(jnp.bfloat16)

    query_blocks = query_heads.reshape(block_count, block_rows, heads_here, HD)
    attended = lax.map(attend, query_blocks).reshape(1, video_len, head_width)
    return lax.all_to_all(attended, "seq", split_axis=1, concat_axis=2, tiled=True)


def solution(mesh):
    placed = (
        P("fsdp", "seq", None, None),
        P("fsdp", "seq", None),
        P("fsdp", None, "seq"),
        P("fsdp", "seq"),
        P("fsdp", "seq"),
        P("fsdp"),
    )
    return jax.shard_map(
        shards, mesh=mesh, in_specs=placed, out_specs=P("fsdp", "seq", None), check_vma=False
    )
```

profile of v0, /device:TPU:4, one launch (start us, length us, event | category | flops | bytes accessed | tf_op | source)
XLA Modules:
  0.0 340.3 jit_solution(14495082860246076433)
XLA Ops:
  6.5 37.7 %all_gather.12 = bf16[8,4096]{1,0:T(8,128)(2,1)} all-gather(bf16[8,256]{1,0:T(8,128)(2,1)} %param.11), channel_id=1, replica_groups=mesh['fsdp'=32,'seq'=16] {'seq'}, dimensions={1}, use_global_device_ids=true | all-gather | bytes 69632 | tf_op jit(solution)/shard_map/all_gather | solution.py:28
  44.2 0.0 all-gather.4.cloned.1.call-update
  44.2 0.0 all-gather.6.cloned.1.call-start
  44.3 0.7 all-gather.6.cloned.1.call-update
  45.0 0.0 slice-start
  45.0 1.6 slice-done
  46.6 3.8 %copy.76 = bf16[1,128,2,4096]{1,2,0,3:T(2,128)(2,1)} copy(bf16[1,128,2,4096]{3,1,2,0:T(8,128)(2,1)S(1)} %slice-done) | data formatting | bytes 4194304
  50.3 3.8 %all-to-all-start.1 = ((bf16[1,128,2,4096]{1,2,0,3:T(2,128)(2,1)}), bf16[1,128,2,4096]{1,2,0,3:T(2,128)(2,1)S(1)}, u32[]{:S(2)}, u32[]{:S(2)}) async-start(bf16[1,128,2,4096]{1,2,0,3:T(2,128)(2,1)} %copy.76), calls=%async_computation.1 | async-start | bytes 4194304 | tf_op jit(solution)/shard_map/all_to_all | solution.py:34
  54.2 0.2 convert_reduce_fusion
  54.4 0.2 fusion.20
  54.6 53.1 %all-gather.4.cloned.1.call-done = bf16[256,4096]{1,0:T(8,128)(2,1)} async-done(((bf16[8,4096]{1,0:T(8,128)(2,1)}), bf16[256,4096]{1,0:T(8,128)(2,1)}) %all-gather.4.cloned.1.call-update) | async-done | bytes 2097168 | tf_op jit(solution)/shard_map/all_gather | solution.py:29
  107.7 2.3 fusion.16
  110.1 3.9 %copy.51 = bf16[1,128,1,4096]{1,2,0,3:T(2,128)(2,1)} copy(bf16[1,128,1,4096]{3,1,2,0:T(8,128)(2,1)S(1)} %fusion.16) | data formatting | bytes 2097152 | tf_op jit(solution)/shard_map/convert_element_type | solution.py:31
  114.0 0.6 broadcast.42
  114.6 23.4 %reduce.1 = bf16[4096,128]{1,0:T(8,128)(2,1)S(1)} reduce(bf16[4096,1,1,128]{3,2,1,0:T(2,128)(2,1)} %bitcast.78, bf16[]{:T(256)} %broadcast.42), dimensions={1,2}, to_apply=%bitcast.56.reduce_sub_computation | reduce | bytes 2097154
  138.0 1.1 reshape.51
  139.2 9.9 %all-to-all-start = ((bf16[16,2,16384]{2,1,0:T(2,128)(2,1)}), bf16[16,2,16384]{2,1,0:T(2,128)(2,1)S(1)}, u32[]{:S(2)}, u32[]{:S(2)}) async-start(bf16[16,2,16384]{2,1,0:T(2,128)(2,1)} %reshape.51), calls=%async_computation | async-start | bytes 2097152 | tf_op jit(solution)/shard_map/all_to_all | solution.py:33
  149.1 0.1 fusion.23
  149.2 58.6 %all-gather = bf16[16,4,5120]{2,1,0:T(4,128)(2,1)} all-gather(bf16[1,4,5120]{2,1,0:T(4,128)(2,1)S(1)} %fusion.23), channel_id=1, replica_groups=mesh['fsdp'=32,'seq'=16] {'seq'}, dimensions={0}, use_global_device_ids=true | all-gather | bytes 696320 | tf_op jit(solution)/shard_map/all_gather | solution.py:37
  207.8 2.3 reshape.49
  210.7 1.6 copy.54
  212.3 2.9 copy.55
  215.2 1.5 fusion.25
  216.7 2.3 copy.56
  219.1 1.4 copy.59
  220.5 1.0 reshape.52
  221.5 0.1 copy.74
  221.7 1.4 copy.52
  223.0 1.3 reshape.44
  224.4 0.0 all-gather.6.cloned.1.call-done
  224.4 3.4 %copy.81 = bf16[640,8,2,256]{3,1,2,0:T(8,128)(2,1)S(1)} copy(bf16[640,8,2,256]{3,2,1,0:T(2,128)(2,1)} %bitcast.82) | data formatting | bytes 10485760
  227.9 1.0 convolution_convert_fusion
  228.9 0.1 fusion.26
  229.0 0.1 copy.69
  229.2 1.4 pad_maximum_fusion
  230.6 1.4 copy.63
  231.9 0.1 copy.70
  232.1 0.1 pad_maximum_fusion.1
  232.2 1.4 copy.64
  233.6 55.6 %while.11 = (s32[]{:T(128)}, bf16[4,512,2,128]{3,2,1,0:T(2,128)(2,1)}, bf16[4,512,2,128]{3,2,1,0:T(2,128)(2,1)S(1)}, bf16[2112,2,128]{2,0,1:T(8,128)(2,1)S(1)}, ...) while((s32[]{:T(128)}, bf16[4,512,2,128]{3,2,1,0:T(2,128)(2,1)}, ...), condition=%wide.region_5.6_spmd.clone, body=%wide.region_2.5_spmd.clone.sunk | while | flops 1122570368 | bytes 25375472 | solution.py:72
  233.6 0.2 constant_dynamic-slice_fusion.2
  233.8 7.4 %fusion.38 = (f32[2,512]{1,0:T(2,128)S(1)}, f32[2,512,2112]{1,2,0:T(8,128)}) fusion(pred[2112]{0:T(1024)(128)(4,1)S(1)} %iota_compare_fusion.4, bf16[2112,2,128]{2,0,1:T(8,128)(2,1)S(1)} %get-tuple-element.153, bf16[1,512,2,128]{3,2,1,0:T(2,128)(2,1)S(1)} %constant_dynamic-slice_fusion.2), kind=kOutput, calls=%fused_computation.38.clone.1 | convolution fusion | flops 564463680 | bytes 10000448 | tf_op jit(solution)/shard_map/while/body/eval_jaxpr/sub | solution.py:65
  241.2 5.3 %fusion.39 = bf16[1,512,2,128]{3,1,2,0:T(8,128)(2,1)S(1)} fusion(bf16[2112,2,128]{2,0,1:T(8,128)(2,1)S(1)} %copy-done.4, f32[2,512,2112]{1,2,0:T(8,128)} %get-tuple-element.134, f32[2,512]{1,0:T(2,128)S(1)} %get-tuple-element.135), kind=kOutput, calls=%fused_computation.11.clone.1 | convolution fusion | flops 558104576 | bytes 9998336 | tf_op jit(solution)/shard_map/while/body/eval_jaxpr/hbk,khd->bhd/dot_general | solution.py:68
  246.5 1.0 copy_dynamic-update-slice_fusion.2
  247.5 0.2 constant_dynamic-slice_fusion.2
  247.7 7.4 %fusion.38 = (f32[2,512]{1,0:T(2,128)S(1)}, f32[2,512,2112]{1,2,0:T(8,128)}) fusion(pred[2112]{0:T(1024)(128)(4,1)S(1)} %iota_compare_fusion.4, bf16[2112,2,128]{2,0,1:T(8,128)(2,1)S(1)} %get-tuple-element.153, bf16[1,512,2,128]{3,2,1,0:T(2,128)(2,1)S(1)} %constant_dynamic-slice_fusion.2), kind=kOutput, calls=%fused_computation.38.clone.1 | convolution fusion | flops 564463680 | bytes 10000448 | tf_op jit(solution)/shard_map/while/body/eval_jaxpr/sub | solution.py:65
  255.1 5.3 %fusion.39 = bf16[1,512,2,128]{3,1,2,0:T(8,128)(2,1)S(1)} fusion(bf16[2112,2,128]{2,0,1:T(8,128)(2,1)S(1)} %copy-done.4, f32[2,512,2112]{1,2,0:T(8,128)} %get-tuple-element.134, f32[2,512]{1,0:T(2,128)S(1)} %get-tuple-element.135), kind=kOutput, calls=%fused_computation.11.clone.1 | convolution fusion | flops 558104576 | bytes 9998336 | tf_op jit(solution)/shard_map/while/body/eval_jaxpr/hbk,khd->bhd/dot_general | solution.py:68
  260.4 1.0 copy_dynamic-update-slice_fusion.2
  261.4 0.2 constant_dynamic-slice_fusion.2
  261.6 7.4 %fusion.38 = (f32[2,512]{1,0:T(2,128)S(1)}, f32[2,512,2112]{1,2,0:T(8,128)}) fusion(pred[2112]{0:T(1024)(128)(4,1)S(1)} %iota_compare_fusion.4, bf16[2112,2,128]{2,0,1:T(8,128)(2,1)S(1)} %get-tuple-element.153, bf16[1,512,2,128]{3,2,1,0:T(2,128)(2,1)S(1)} %constant_dynamic-slice_fusion.2), kind=kOutput, calls=%fused_computation.38.clone.1 | convolution fusion | flops 564463680 | bytes 10000448 | tf_op jit(solution)/shard_map/while/body/eval_jaxpr/sub | solution.py:65
  269.0 5.3 %fusion.39 = bf16[1,512,2,128]{3,1,2,0:T(8,128)(2,1)S(1)} fusion(bf16[2112,2,128]{2,0,1:T(8,128)(2,1)S(1)} %copy-done.4, f32[2,512,2112]{1,2,0:T(8,128)} %get-tuple-element.134, f32[2,512]{1,0:T(2,128)S(1)} %get-tuple-element.135), kind=kOutput, calls=%fused_computation.11.clone.1 | convolution fusion | flops 558104576 | bytes 9998336 | tf_op jit(solution)/shard_map/while/body/eval_jaxpr/hbk,khd->bhd/dot_general | solution.py:68
  274.3 1.0 copy_dynamic-update-slice_fusion.2
  275.3 0.2 constant_dynamic-slice_fusion.2
  275.5 7.4 %fusion.38 = (f32[2,512]{1,0:T(2,128)S(1)}, f32[2,512,2112]{1,2,0:T(8,128)}) fusion(pred[2112]{0:T(1024)(128)(4,1)S(1)} %iota_compare_fusion.4, bf16[2112,2,128]{2,0,1:T(8,128)(2,1)S(1)} %get-tuple-element.153, bf16[1,512,2,128]{3,2,1,0:T(2,128)(2,1)S(1)} %constant_dynamic-slice_fusion.2), kind=kOutput, calls=%fused_computation.38.clone.1 | convolution fusion | flops 564463680 | bytes 10000448 | tf_op jit(solution)/shard_map/while/body/eval_jaxpr/sub | solution.py:65
  282.9 5.3 %fusion.39 = bf16[1,512,2,128]{3,1,2,0:T(8,128)(2,1)S(1)} fusion(bf16[2112,2,128]{2,0,1:T(8,128)(2,1)S(1)} %copy-done.4, f32[2,512,2112]{1,2,0:T(8,128)} %get-tuple-element.134, f32[2,512]{1,0:T(2,128)S(1)} %get-tuple-element.135), kind=kOutput, calls=%fused_computation.11.clone.1 | convolution fusion | flops 558104576 | bytes 9998336 | tf_op jit(solution)/shard_map/while/body/eval_jaxpr/hbk,khd->bhd/dot_general | solution.py:68
  288.2 1.0 copy_dynamic-update-slice_fusion.2
  289.2 6.6 %reshape.50 = bf16[1,2048,256]{2,0,1:T(2,128)(2,1)S(1)} reshape(bf16[4,512,2,128]{3,2,1,0:T(2,128)(2,1)} %get-tuple-element.37) | data formatting | bytes 2097152 | tf_op jit(solution)/shard_map/reshape | solution.py:72
  295.8 10.6 %reduce.2 = bf16[2048,256]{1,0:T(8,128)(2,1)S(1)} reduce(bf16[2048,1,256]{2,1,0:T(2,128)(2,1)S(1)} %bitcast.80, bf16[]{:T(256)} %broadcast.42), dimensions={1}, to_apply=%bitcast.58.reduce_sub_computation | reduce | bytes 2097154
  306.4 0.3 reshape.53
  306.7 23.5 %all_to_all.51 = bf16[16,2,16384]{2,1,0:T(2,128)(2,1)S(1)} all-to-all(bf16[16,2,16384]{2,1,0:T(2,128)(2,1)S(1)} %reshape.53), channel_id=1, replica_groups=mesh['fsdp'=32,'seq'=16] {'seq'}, dimensions={0} | all-to-all | bytes 2097152 | tf_op jit(solution)/shard_map/all_to_all | solution.py:73
  330.2 1.0 reshape.54
  331.2 0.2 copy.75
  331.4 0.7 copy.67
  332.1 1.3 copy.68
  (31 shorter events, 0.1 us)
Async XLA Ops:
  6.5 101.2 %all-gather.4.cloned.1.call-start = ((), (), s32[]{:S(2)}) async-start(), calls=%async_computation.3 | async-start | bytes 2162688 | tf_op jit(solution)/shard_map/all_gather | solution.py:29
  44.2 180.2 %all-gather.6.cloned.1.call-start = ((), (), s32[]{:S(2)}) async-start(), calls=%async_computation.4 | async-start | bytes 5406720 | tf_op jit(solution)/shard_map/all_gather | solution.py:40
  45.0 1.6 slice-start
  50.3 3.9 %copy-start.5 = (bf16[1,4,5120]{2,1,0:T(4,128)(2,1)S(1)}, bf16[1,4,5120]{2,1,0:T(4,128)(2,1)}, u32[]{:S(2)}) copy-start(bf16[1,4,5120]{2,1,0:T(4,128)(2,1)} %param.9) | copy-start | bytes 122884
  50.3 57.4 %copy-start.6 = (s32[1,128]{1,0:T(1,128)S(1)}, s32[1,128]{1,0:T(1,128)}, u32[]{:S(2)}) copy-start(s32[1,128]{1,0:T(1,128)} %param.12) | copy-start | bytes 1540
  50.3 88.8 %all-to-all-start.1 = ((bf16[1,128,2,4096]{1,2,0,3:T(2,128)(2,1)}), bf16[1,128,2,4096]{1,2,0,3:T(2,128)(2,1)S(1)}, u32[]{:S(2)}, u32[]{:S(2)}) async-start(bf16[1,128,2,4096]{1,2,0,3:T(2,128)(2,1)} %copy.76), calls=%async_computation.1 | async-start | bytes 4194304 | tf_op jit(solution)/shard_map/all_to_all | solution.py:34
  139.2 81.3 %all-to-all-start = ((bf16[16,2,16384]{2,1,0:T(2,128)(2,1)}), bf16[16,2,16384]{2,1,0:T(2,128)(2,1)S(1)}, u32[]{:S(2)}, u32[]{:S(2)}) async-start(bf16[16,2,16384]{2,1,0:T(2,128)(2,1)} %reshape.51), calls=%async_computation | async-start | bytes 2097152 | tf_op jit(solution)/shard_map/all_to_all | solution.py:33
  216.7 2.3 copy-start.1
  224.4 3.4 %copy-start.2 = (bf16[64,5120]{1,0:T(8,128)(2,1)S(1)}, bf16[64,5120]{1,0:T(8,128)(2,1)}, u32[]{:S(2)}) copy-start(bf16[64,5120]{1,0:T(8,128)(2,1)} %reshape.49) | copy-start | bytes 1966084
  229.2 2.9 copy-start
  232.2 1.4 copy-start.3
  233.8 7.4 %copy-start.4 = (bf16[2112,2,128]{2,0,1:T(8,128)(2,1)S(1)}, bf16[2112,2,128]{2,0,1:T(8,128)(2,1)}, u32[]{:S(2)}) copy-start(bf16[2112,2,128]{2,0,1:T(8,128)(2,1)} %get-tuple-element.154) | copy-start | bytes 3244036 | tf_op jit(solution)/shard_map/while
  247.7 7.4 %copy-start.4 = (bf16[2112,2,128]{2,0,1:T(8,128)(2,1)S(1)}, bf16[2112,2,128]{2,0,1:T(8,128)(2,1)}, u32[]{:S(2)}) copy-start(bf16[2112,2,128]{2,0,1:T(8,128)(2,1)} %get-tuple-element.154) | copy-start | bytes 3244036 | tf_op jit(solution)/shard_map/while
  261.6 7.4 %copy-start.4 = (bf16[2112,2,128]{2,0,1:T(8,128)(2,1)S(1)}, bf16[2112,2,128]{2,0,1:T(8,128)(2,1)}, u32[]{:S(2)}) copy-start(bf16[2112,2,128]{2,0,1:T(8,128)(2,1)} %get-tuple-element.154) | copy-start | bytes 3244036 | tf_op jit(solution)/shard_map/while
  275.5 7.4 %copy-start.4 = (bf16[2112,2,128]{2,0,1:T(8,128)(2,1)S(1)}, bf16[2112,2,128]{2,0,1:T(8,128)(2,1)}, u32[]{:S(2)}) copy-start(bf16[2112,2,128]{2,0,1:T(8,128)(2,1)} %get-tuple-element.154) | copy-start | bytes 3244036 | tf_op jit(solution)/shard_map/while
Sparse Core Ops, SparseCore 0:
  44.3 63.3 all-gather.3
  110.9 82.3 all-gather.5
where the time goes:
time: 341 us; the launch traced here: 340 us
  blocking collectives  120 us (35%)
  matrix products  54.2 us (16%)
  waiting for transfers between devices  53.9 us (16%)
  local copies, waits for them, and re-layouts  48.2 us (14%)
  other arithmetic  36 us (11%)
  between operations  14.3 us (4%)
  starting transfers between devices  13.8 us (4%)
    all_gather x1, blocking collectives, shards(): all_rows = lax.all_gather(normed, 'seq', axis=0, tiled=True)  58.6 us
    all_gather x1, waiting for transfers between devices, shards(): codebook = lax.all_gather(codebook_cols, 'fsdp', axis=0, tiled=True)  53.1 us
    all_gather x1, blocking collectives, shards(): codebook_cols = lax.all_gather(pose_table, 'seq', axis=1, tiled=True)  37.7 us
    unnamed x3, other arithmetic  34.1 us
    sub x4, matrix products, attend(): expo = jnp.where(live_keys[None, None, :], jnp.exp(scores - row_max), 0.0)  29.5 us
    all_to_all x1, blocking collectives, shards(): lax.all_to_all(attended, 'seq', split_axis=1, concat_axis=2, tiled=True)  23.5 us
    dot_general x4, matrix products, attend(): jnp.einsum('hbk,khd->bhd', weights, value_rows, preferred_element_type=jn...  21.3 us
    unnamed x24, local copies, waits for them, and re-layouts  16.6 us
  transfers between devices with their start and end apart: 4, of which 1 were waited for; matrix products, arithmetic and copies ran while one was open for 15% of the time, Pallas kernels for 0%

commit v1 on v0

--- a/solution.py
+++ b/solution.py
@@ -70,7 +70,10 @@
 
     query_blocks = query_heads.reshape(block_count, block_rows, heads_here, HD)
     attended = lax.map(attend, query_blocks).reshape(1, video_len, head_width)
-    return lax.all_to_all(attended, "seq", split_axis=1, concat_axis=2, tiled=True)
+    return jnp.concatenate(
+        lax.all_to_all(jnp.stack(jnp.split(attended, lax.axis_size("seq"), axis=1)), "seq", 0, 0),
+        axis=2,
+    )
 
 
 def solution(mesh):

time: 341 us -> 324 us (0.950)
  the two profiles are of different devices: /device:TPU:4 before, /device:TPU:2 now
where the time goes in v1:
time: 324 us; the launch traced here: 323 us
  blocking collectives  120 us (37%)
  matrix products  54.2 us (17%)
  waiting for transfers between devices  54 us (17%)
  local copies, waits for them, and re-layouts  41.2 us (13%)
  other arithmetic  25.4 us (8%)
  between operations  14.4 us (4%)
  starting transfers between devices  13.2 us (4%)
    all_gather x1, blocking collectives, shards(): all_rows = lax.all_gather(normed, 'seq', axis=0, tiled=True)  58.9 us
    all_gather x1, waiting for transfers between devices, shards(): codebook = lax.all_gather(codebook_cols, 'fsdp', axis=0, tiled=True)  53.3 us
    all_gather x1, blocking collectives, shards(): codebook_cols = lax.all_gather(pose_table, 'seq', axis=1, tiled=True)  37.7 us
    sub x4, matrix products, attend(): expo = jnp.where(live_keys[None, None, :], jnp.exp(scores - row_max), 0.0)  29.5 us
    all_to_all x1, blocking collectives, shards(): lax.all_to_all(jnp.stack(jnp.split(attended, lax.axis_size('seq'), axis=1...  23.7 us
    unnamed x2, other arithmetic  23.5 us
    dot_general x4, matrix products, attend(): jnp.einsum('hbk,khd->bhd', weights, value_rows, preferred_element_type=jn...  21.3 us
    unnamed x36, local copies, waits for them, and re-layouts  15.2 us
  transfers between devices with their start and end apart: 4, of which 1 were waited for; matrix products, arithmetic and copies ran while one was open for 16% of the time, Pallas kernels for 0%

profile of v1, /device:TPU:2, one launch (start us, length us, event | category | flops | bytes accessed | tf_op | source)
XLA Modules:
  0.0 322.8 jit_solution(14775819270442076817)
XLA Ops:
  6.5 37.7 %all_gather.12 = bf16[8,4096]{1,0:T(8,128)(2,1)} all-gather(bf16[8,256]{1,0:T(8,128)(2,1)} %param.11), channel_id=1, replica_groups=mesh['fsdp'=32,'seq'=16] {'seq'}, dimensions={1}, use_global_device_ids=true | all-gather | bytes 69632 | tf_op jit(solution)/shard_map/all_gather | solution.py:28
  44.2 0.0 all-gather.4.cloned.1.call-update
  44.2 0.0 slice-start
  44.2 0.0 all-gather.6.cloned.1.call-start
  44.3 0.7 all-gather.6.cloned.1.call-update
  45.0 0.8 slice-done
  45.8 3.8 %copy.88 = bf16[1,128,2,4096]{1,2,0,3:T(2,128)(2,1)} copy(bf16[1,128,2,4096]{3,1,2,0:T(8,128)(2,1)S(1)} %slice-done) | data formatting | bytes 4194304
  49.6 3.8 %all-to-all-start.1 = ((bf16[1,128,2,4096]{1,2,0,3:T(2,128)(2,1)}), bf16[1,128,2,4096]{1,2,0,3:T(2,128)(2,1)S(1)}, u32[]{:S(2)}, u32[]{:S(2)}) async-start(bf16[1,128,2,4096]{1,2,0,3:T(2,128)(2,1)} %copy.88), calls=%async_computation.1 | async-start | bytes 4194304 | tf_op jit(solution)/shard_map/all_to_all | solution.py:34
  53.5 0.0 copy-done.5
  53.5 0.2 convert_reduce_fusion
  53.7 0.2 fusion.20
  53.9 53.3 %all-gather.4.cloned.1.call-done = bf16[256,4096]{1,0:T(8,128)(2,1)} async-done(((bf16[8,4096]{1,0:T(8,128)(2,1)}), bf16[256,4096]{1,0:T(8,128)(2,1)}) %all-gather.4.cloned.1.call-update) | async-done | bytes 2097168 | tf_op jit(solution)/shard_map/all_gather | solution.py:29
  107.2 0.0 copy-done.6
  107.2 2.3 fusion.16
  109.5 3.9 %copy.65 = bf16[1,128,1,4096]{1,2,0,3:T(2,128)(2,1)} copy(bf16[1,128,1,4096]{3,1,2,0:T(8,128)(2,1)S(1)} %fusion.16) | data formatting | bytes 2097152 | tf_op jit(solution)/shard_map/convert_element_type | solution.py:31
  113.4 0.5 broadcast.42
  113.9 23.4 %reduce.1 = bf16[4096,128]{1,0:T(8,128)(2,1)S(1)} reduce(bf16[4096,1,1,128]{3,2,1,0:T(2,128)(2,1)} %bitcast.137, bf16[]{:T(256)} %broadcast.42), dimensions={1,2}, to_apply=%bitcast.118.reduce_sub_computation | reduce | bytes 2097154
  137.4 1.2 reshape.58
  138.5 0.0 all-to-all-done.1
  138.5 9.3 %all-to-all-start = ((bf16[16,2,16384]{2,1,0:T(2,128)(2,1)}), bf16[16,2,16384]{2,1,0:T(2,128)(2,1)S(1)}, u32[]{:S(2)}, u32[]{:S(2)}) async-start(bf16[16,2,16384]{2,1,0:T(2,128)(2,1)} %reshape.58), calls=%async_computation | async-start | bytes 2097152 | tf_op jit(solution)/shard_map/all_to_all | solution.py:33
  147.9 0.1 fusion.39
  148.0 58.9 %all-gather = bf16[16,4,5120]{2,1,0:T(4,128)(2,1)} all-gather(bf16[1,4,5120]{2,1,0:T(4,128)(2,1)S(1)} %fusion.39), channel_id=1, replica_groups=mesh['fsdp'=32,'seq'=16] {'seq'}, dimensions={0}, use_global_device_ids=true | all-gather | bytes 696320 | tf_op jit(solution)/shard_map/all_gather | solution.py:37
  206.9 2.3 reshape.57
  209.8 1.6 copy.68
  211.4 2.9 copy.69
  214.3 1.5 fusion.41
  215.8 2.3 copy.70
  218.1 1.4 copy.73
  219.6 0.0 all-to-all-done
  219.6 1.0 reshape.59
  220.6 0.1 copy.87
  220.8 1.4 copy.66
  222.1 1.3 reshape.50
  223.5 0.0 all-gather.6.cloned.1.call-done
  223.5 3.4 %copy.93 = bf16[640,8,2,256]{3,1,2,0:T(8,128)(2,1)S(1)} copy(bf16[640,8,2,256]{3,2,1,0:T(2,128)(2,1)} %bitcast.140) | data formatting | bytes 10485760
  227.0 1.0 convolution_convert_fusion
  228.0 0.1 fusion.42
  228.1 0.1 copy.82
  228.3 1.4 pad_maximum_fusion
  229.7 1.3 copy.77
  231.0 0.1 copy.83
  231.1 0.1 pad_maximum_fusion.1
  231.3 1.4 copy.78
  232.7 55.7 %while.11 = (s32[]{:T(128)}, bf16[4,512,2,128]{3,2,1,0:T(2,128)(2,1)}, bf16[4,512,2,128]{3,2,1,0:T(2,128)(2,1)S(1)}, bf16[2112,2,128]{2,0,1:T(8,128)(2,1)S(1)}, ...) while((s32[]{:T(128)}, bf16[4,512,2,128]{3,2,1,0:T(2,128)(2,1)}, ...), condition=%wide.region_5.6_spmd.clone, body=%wide.region_2.5_spmd.clone.sunk | while | flops 1122570368 | bytes 25375472 | solution.py:72
  232.7 0.2 constant_dynamic-slice_fusion.2
  232.9 7.4 %fusion.54 = (f32[2,512]{1,0:T(2,128)S(1)}, f32[2,512,2112]{1,2,0:T(8,128)}) fusion(pred[2112]{0:T(1024)(128)(4,1)S(1)} %iota_compare_fusion.4, bf16[2112,2,128]{2,0,1:T(8,128)(2,1)S(1)} %get-tuple-element.153, bf16[1,512,2,128]{3,2,1,0:T(2,128)(2,1)S(1)} %constant_dynamic-slice_fusion.2), kind=kOutput, calls=%fused_computation.70.clone.1 | convolution fusion | flops 564463680 | bytes 10000448 | tf_op jit(solution)/shard_map/while/body/eval_jaxpr/sub | solution.py:65
  240.3 5.3 %fusion.55 = bf16[1,512,2,128]{3,1,2,0:T(8,128)(2,1)S(1)} fusion(bf16[2112,2,128]{2,0,1:T(8,128)(2,1)S(1)} %copy-done.4, f32[2,512,2112]{1,2,0:T(8,128)} %get-tuple-element.134, f32[2,512]{1,0:T(2,128)S(1)} %get-tuple-element.135), kind=kOutput, calls=%fused_computation.11.clone.1 | convolution fusion | flops 558104576 | bytes 9998336 | tf_op jit(solution)/shard_map/while/body/eval_jaxpr/hbk,khd->bhd/dot_general | solution.py:68
  245.6 1.0 copy_dynamic-update-slice_fusion.2
  246.6 0.2 constant_dynamic-slice_fusion.2
  246.8 7.4 %fusion.54 = (f32[2,512]{1,0:T(2,128)S(1)}, f32[2,512,2112]{1,2,0:T(8,128)}) fusion(pred[2112]{0:T(1024)(128)(4,1)S(1)} %iota_compare_fusion.4, bf16[2112,2,128]{2,0,1:T(8,128)(2,1)S(1)} %get-tuple-element.153, bf16[1,512,2,128]{3,2,1,0:T(2,128)(2,1)S(1)} %constant_dynamic-slice_fusion.2), kind=kOutput, calls=%fused_computation.70.clone.1 | convolution fusion | flops 564463680 | bytes 10000448 | tf_op jit(solution)/shard_map/while/body/eval_jaxpr/sub | solution.py:65
  254.2 5.3 %fusion.55 = bf16[1,512,2,128]{3,1,2,0:T(8,128)(2,1)S(1)} fusion(bf16[2112,2,128]{2,0,1:T(8,128)(2,1)S(1)} %copy-done.4, f32[2,512,2112]{1,2,0:T(8,128)} %get-tuple-element.134, f32[2,512]{1,0:T(2,128)S(1)} %get-tuple-element.135), kind=kOutput, calls=%fused_computation.11.clone.1 | convolution fusion | flops 558104576 | bytes 9998336 | tf_op jit(solution)/shard_map/while/body/eval_jaxpr/hbk,khd->bhd/dot_general | solution.py:68
  259.5 1.0 copy_dynamic-update-slice_fusion.2
  260.5 0.2 constant_dynamic-slice_fusion.2
  260.7 7.4 %fusion.54 = (f32[2,512]{1,0:T(2,128)S(1)}, f32[2,512,2112]{1,2,0:T(8,128)}) fusion(pred[2112]{0:T(1024)(128)(4,1)S(1)} %iota_compare_fusion.4, bf16[2112,2,128]{2,0,1:T(8,128)(2,1)S(1)} %get-tuple-element.153, bf16[1,512,2,128]{3,2,1,0:T(2,128)(2,1)S(1)} %constant_dynamic-slice_fusion.2), kind=kOutput, calls=%fused_computation.70.clone.1 | convolution fusion | flops 564463680 | bytes 10000448 | tf_op jit(solution)/shard_map/while/body/eval_jaxpr/sub | solution.py:65
  268.1 5.3 %fusion.55 = bf16[1,512,2,128]{3,1,2,0:T(8,128)(2,1)S(1)} fusion(bf16[2112,2,128]{2,0,1:T(8,128)(2,1)S(1)} %copy-done.4, f32[2,512,2112]{1,2,0:T(8,128)} %get-tuple-element.134, f32[2,512]{1,0:T(2,128)S(1)} %get-tuple-element.135), kind=kOutput, calls=%fused_computation.11.clone.1 | convolution fusion | flops 558104576 | bytes 9998336 | tf_op jit(solution)/shard_map/while/body/eval_jaxpr/hbk,khd->bhd/dot_general | solution.py:68
  273.4 1.0 copy_dynamic-update-slice_fusion.2
  274.4 0.2 constant_dynamic-slice_fusion.2
  274.6 7.4 %fusion.54 = (f32[2,512]{1,0:T(2,128)S(1)}, f32[2,512,2112]{1,2,0:T(8,128)}) fusion(pred[2112]{0:T(1024)(128)(4,1)S(1)} %iota_compare_fusion.4, bf16[2112,2,128]{2,0,1:T(8,128)(2,1)S(1)} %get-tuple-element.153, bf16[1,512,2,128]{3,2,1,0:T(2,128)(2,1)S(1)} %constant_dynamic-slice_fusion.2), kind=kOutput, calls=%fused_computation.70.clone.1 | convolution fusion | flops 564463680 | bytes 10000448 | tf_op jit(solution)/shard_map/while/body/eval_jaxpr/sub | solution.py:65
  282.0 5.3 %fusion.55 = bf16[1,512,2,128]{3,1,2,0:T(8,128)(2,1)S(1)} fusion(bf16[2112,2,128]{2,0,1:T(8,128)(2,1)S(1)} %copy-done.4, f32[2,512,2112]{1,2,0:T(8,128)} %get-tuple-element.134, f32[2,512]{1,0:T(2,128)S(1)} %get-tuple-element.135), kind=kOutput, calls=%fused_computation.11.clone.1 | convolution fusion | flops 558104576 | bytes 9998336 | tf_op jit(solution)/shard_map/while/body/eval_jaxpr/hbk,khd->bhd/dot_general | solution.py:68
  287.3 1.0 copy_dynamic-update-slice_fusion.2
  288.3 1.7 reshape.53
  290.3 23.7 %all_to_all.38 = bf16[16,1,128,256]{3,2,1,0:T(8,128)(2,1)S(1)} all-to-all(bf16[16,1,128,256]{3,2,1,0:T(8,128)(2,1)S(1)} %fusion.22), channel_id=1, replica_groups=mesh['fsdp'=32,'seq'=16] {'seq'}, dimensions={0} | all-to-all | bytes 2097152 | tf_op jit(solution)/shard_map/all_to_all | solution.py:74
  314.0 0.7 copy.80
  314.7 1.3 copy.81
  (43 shorter events, 0.2 us)
Async XLA Ops:
  6.5 100.6 %all-gather.4.cloned.1.call-start = ((), (), s32[]{:S(2)}) async-start(), calls=%async_computation.3 | async-start | bytes 2162688 | tf_op jit(solution)/shard_map/all_gather | solution.py:29
  44.2 1.6 slice-start
  44.2 179.3 %all-gather.6.cloned.1.call-start = ((), (), s32[]{:S(2)}) async-start(), calls=%async_computation.4 | async-start | bytes 5406720 | tf_op jit(solution)/shard_map/all_gather | solution.py:40
  49.6 3.9 %copy-start.5 = (bf16[1,4,5120]{2,1,0:T(4,128)(2,1)S(1)}, bf16[1,4,5120]{2,1,0:T(4,128)(2,1)}, u32[]{:S(2)}) copy-start(bf16[1,4,5120]{2,1,0:T(4,128)(2,1)} %param.9) | copy-start | bytes 122884
  49.6 57.5 %copy-start.6 = (s32[1,128]{1,0:T(1,128)S(1)}, s32[1,128]{1,0:T(1,128)}, u32[]{:S(2)}) copy-start(s32[1,128]{1,0:T(1,128)} %param.12) | copy-start | bytes 1540
  49.6 88.9 %all-to-all-start.1 = ((bf16[1,128,2,4096]{1,2,0,3:T(2,128)(2,1)}), bf16[1,128,2,4096]{1,2,0,3:T(2,128)(2,1)S(1)}, u32[]{:S(2)}, u32[]{:S(2)}) async-start(bf16[1,128,2,4096]{1,2,0,3:T(2,128)(2,1)} %copy.88), calls=%async_computation.1 | async-start | bytes 4194304 | tf_op jit(solution)/shard_map/all_to_all | solution.py:34
  138.5 81.0 %all-to-all-start = ((bf16[16,2,16384]{2,1,0:T(2,128)(2,1)}), bf16[16,2,16384]{2,1,0:T(2,128)(2,1)S(1)}, u32[]{:S(2)}, u32[]{:S(2)}) async-start(bf16[16,2,16384]{2,1,0:T(2,128)(2,1)} %reshape.58), calls=%async_computation | async-start | bytes 2097152 | tf_op jit(solution)/shard_map/all_to_all | solution.py:33
  215.8 2.4 copy-start.1
  223.5 3.4 %copy-start.2 = (bf16[64,5120]{1,0:T(8,128)(2,1)S(1)}, bf16[64,5120]{1,0:T(8,128)(2,1)}, u32[]{:S(2)}) copy-start(bf16[64,5120]{1,0:T(8,128)(2,1)} %reshape.57) | copy-start | bytes 1966084
  228.2 2.9 copy-start
  231.2 1.4 copy-start.3
  232.9 7.4 %copy-start.4 = (bf16[2112,2,128]{2,0,1:T(8,128)(2,1)S(1)}, bf16[2112,2,128]{2,0,1:T(8,128)(2,1)}, u32[]{:S(2)}) copy-start(bf16[2112,2,128]{2,0,1:T(8,128)(2,1)} %get-tuple-element.154) | copy-start | bytes 3244036 | tf_op jit(solution)/shard_map/while
  246.8 7.4 %copy-start.4 = (bf16[2112,2,128]{2,0,1:T(8,128)(2,1)S(1)}, bf16[2112,2,128]{2,0,1:T(8,128)(2,1)}, u32[]{:S(2)}) copy-start(bf16[2112,2,128]{2,0,1:T(8,128)(2,1)} %get-tuple-element.154) | copy-start | bytes 3244036 | tf_op jit(solution)/shard_map/while
  260.7 7.4 %copy-start.4 = (bf16[2112,2,128]{2,0,1:T(8,128)(2,1)S(1)}, bf16[2112,2,128]{2,0,1:T(8,128)(2,1)}, u32[]{:S(2)}) copy-start(bf16[2112,2,128]{2,0,1:T(8,128)(2,1)} %get-tuple-element.154) | copy-start | bytes 3244036 | tf_op jit(solution)/shard_map/while
  274.6 7.4 %copy-start.4 = (bf16[2112,2,128]{2,0,1:T(8,128)(2,1)S(1)}, bf16[2112,2,128]{2,0,1:T(8,128)(2,1)}, u32[]{:S(2)}) copy-start(bf16[2112,2,128]{2,0,1:T(8,128)(2,1)} %get-tuple-element.154) | copy-start | bytes 3244036 | tf_op jit(solution)/shard_map/while
Sparse Core Ops, SparseCore 0:
  44.3 62.7 all-gather.3
  110.3 82.6 all-gather.5
